TPU v7x, 128 devices: a whole 4x4x4 slice. The times are simulated.
128 devices in a mesh: dp: 16 (over y, x), inner: 8 (over z, core).
Axes of the slice: x: 4, y: 4, z: 4, core: 2. Of those that a mesh axis runs over, the one named last changes fastest.
Arguments:
- queries: bfloat16 [64, 512, 1024], P('dp', 'inner'), may hold values from -6 to 6
- passages: bfloat16 [64, 512, 1024], P('dp', 'inner'), may hold values from -6 to 6
- neg_lists: int32 [64, 8], replicated, may hold values from 0 to 63, as said below
Outputs:
- mean_loss: float32 [], replicated
- query_grad: bfloat16 [64, 512, 1024], P('dp', 'inner')
- passage_grad: bfloat16 [64, 512, 1024], P('dp', 'inner')
Inputs may be any that keep to these rules, and one draw needn't show every extreme that they name: `neg_lists`: each row lists 8 different passage blocks, none from the row's own group (blocks with the same id // 4). The blocks that the rows of one group list include at least one and at most 2 blocks of every other group; in every draw some group lists exactly 2 blocks of every other group.
All inputs are finite; a program needn't handle non-finite values.
Results may differ from a plain program's by a relative error of at most 0.009.
Values may be sent and summed in bfloat16 or wider, within the bound.
A program may use at most 128 MiB of HBM per device.

v0:
```python
import math
import jax
import jax.numpy as jnp
from jax import lax
from jax.sharding import PartitionSpec as P

CAP = 2
NEG_FILL = -1e30


def slot_tables(neg_lists, groups, per_group, slot_depth):
    block_count = neg_lists.shape[0]
    block_ids = jnp.arange(block_count, dtype=jnp.int32)
    named = jnp.any(neg_lists[:, :, None] == block_ids[None, None, :], axis=1)
    present = jnp.any(named.reshape(groups, per_group, block_count), axis=1)
    present = present.reshape(groups, groups, per_group).astype(jnp.int32)
    slot_ranks = jnp.cumsum(present, axis=2) - 1
    slot_ids = jnp.arange(slot_depth, dtype=jnp.int32)
    hits = (present[..., None] == 1) & (slot_ranks[..., None] == slot_ids[None, None, None, :])
    local_ids = jnp.arange(per_group, dtype=jnp.int32)
    slot_block = jnp.sum(jnp.where(hits, local_ids[None, None, :, None], 0), axis=2)
    slot_live = jnp.any(hits, axis=2)
    return (slot_ranks, slot_block, slot_live)


def body(queries, passages, neg_lists):
    per_group, slice_rows, embed_width = queries.shape
    pick_count = neg_lists.shape[1]
    groups = lax.axis_size("dp")
    inner_count = lax.axis_size("inner")
    full_rows = slice_rows * inner_count
    cand_rows = (pick_count + 1) * slice_rows
    slot_count = groups * CAP
    score_scale = 1.0 / math.sqrt(embed_width)
    my_group = lax.axis_index("dp")
    inner_pos = lax.axis_index("inner")
    slot_ranks, slot_block, slot_live = slot_tables(neg_lists, groups, per_group, CAP)
    listed = lax.dynamic_slice_in_dim(neg_lists, my_group * per_group, per_group, 0)
    owner_group = listed // per_group
    owner_local = listed % per_group
    my_ranks = lax.dynamic_index_in_dim(slot_ranks, my_group, 0, keepdims=False)
    slot_of = owner_group * CAP + my_ranks[owner_group, owner_local]
    sends_for = lax.dynamic_index_in_dim(slot_block, my_group, 1, keepdims=False)
    live_for = lax.dynamic_index_in_dim(slot_live, my_group, 1, keepdims=False)
    block_ids = jnp.arange(per_group, dtype=jnp.int32)
    held_start = jnp.zeros((per_group, pick_count, slice_rows, embed_width), jnp.bfloat16)
    shard_rows = lax.all_gather(passages, "dp", axis=0, tiled=True)
    inside = (listed >= 0) & (listed < shard_rows.shape[0])
    picked = shard_rows[jnp.clip(listed, 0, shard_rows.shape[0] - 1)]
    negatives = jnp.where(inside[:, :, None, None], picked, held_start)
    whole_queries = lax.all_gather(queries, "inner", axis=1, tiled=True)

    def candidates(block_index):
        own_rows = lax.dynamic_index_in_dim(passages, block_index, 0, keepdims=True)
        other_rows = lax.dynamic_index_in_dim(negatives, block_index, 0, keepdims=False)
        return jnp.concatenate([own_rows, other_rows], axis=0).reshape(cand_rows, embed_width)

    def scores(block_index, query_block):
        return (
            jnp.einsum(
                "cd,rd->cr",
                candidates(block_index),
                query_block,
                preferred_element_type=jnp.float32,
            )
            * score_scale
        )

    def forward(inputs):
        block_index, query_block = inputs
        logits = scores(block_index, query_block)
        row_peak = jnp.max(logits, axis=0)
        row_mass = jnp.sum(jnp.exp(logits - row_peak[None, :]), axis=0)
        col_peak = jnp.max(logits, axis=1)
        col_mass = jnp.sum(jnp.exp(logits - col_peak[:, None]), axis=1)
        return (row_peak, row_mass, col_peak, col_mass)

    row_peak, row_mass, col_peak, col_mass = lax.map(forward, (block_ids, whole_queries))
    peak_all = lax.pmax(row_peak, "inner")
    mass_all = lax.psum(row_mass * jnp.exp(row_peak - peak_all), "inner")
    query_lse = peak_all + jnp.log(mass_all)
    own_peak = col_peak[:, :slice_rows]
    own_mass = col_mass[:, :slice_rows]
    far_peak = col_peak[:, slice_rows:].reshape(per_group * pick_count, slice_rows)
    far_mass = col_mass[:, slice_rows:].reshape(per_group * pick_count, slice_rows)
    flat_slots = slot_of.reshape(-1)
    onehot = flat_slots[:, None] == jnp.arange(slot_count, dtype=jnp.int32)[None, :]
    slot_peak = jnp.max(jnp.where(onehot[:, :, None], far_peak[:, None, :], NEG_FILL), axis=0)
    rescaled = far_mass * jnp.exp(far_peak - slot_peak[flat_slots])
    slot_mass = jnp.dot(onehot.astype(jnp.float32).T, rescaled, precision=lax.Precision.HIGHEST)
    got_peak, got_mass = (
        lax.all_to_all(
            slot_peak.reshape(groups, CAP, slice_rows),
            "dp",
            split_axis=0,
            concat_axis=0,
            tiled=True,
        ),
        lax.all_to_all(
            slot_mass.reshape(groups, CAP, slice_rows),
            "dp",
            split_axis=0,
            concat_axis=0,
            tiled=True,
        ),
    )
    belongs = (sends_for[:, :, None] == block_ids[None, None, :]) & live_for[:, :, None]
    belongs = belongs.reshape(slot_count, per_group)
    got_peak = got_peak.reshape(slot_count, slice_rows)
    got_mass = got_mass.reshape(slot_count, slice_rows)
    spread_peak = jnp.where(belongs[:, :, None], got_peak[:, None, :], NEG_FILL)
    pass_peak = jnp.maximum(own_peak, jnp.max(spread_peak, axis=0))
    spread_mass = jnp.where(
        belongs[:, :, None],
        got_mass[:, None, :] * jnp.exp(spread_peak - pass_peak[None, :, :]),
        0.0,
    )
    pass_mass = own_mass * jnp.exp(own_peak - pass_peak) + jnp.sum(spread_mass, axis=0)
    passage_lse = pass_peak + jnp.log(pass_mass)
    own_scores = (
        jnp.einsum("lrd,lrd->lr", queries, passages, preferred_element_type=jnp.float32)
        * score_scale
    )
    my_query_lse = lax.dynamic_slice_in_dim(query_lse, inner_pos * slice_rows, slice_rows, 1)
    local_loss = jnp.sum(my_query_lse - own_scores) + jnp.sum(passage_lse - own_scores)
    mean_loss = lax.psum(local_loss, ("dp", "inner")) / (2.0 * groups * per_group * full_rows)
    lse_out = passage_lse[sends_for]
    lse_back = lax.all_to_all(lse_out, "dp", split_axis=0, concat_axis=0, tiled=True).reshape(
        slot_count, slice_rows
    )
    cand_lse = jnp.concatenate([passage_lse[:, None, :], lse_back[slot_of]], axis=1).reshape(
        per_group, cand_rows
    )
    cand_pos = jnp.arange(cand_rows, dtype=jnp.int32)
    row_pos = jnp.arange(full_rows, dtype=jnp.int32)
    target = (
        (cand_pos[:, None] < slice_rows)
        & (row_pos[None, :] == inner_pos * slice_rows + cand_pos[:, None])
    ).astype(jnp.float32)

    def backward(block_index, carry):
        weights, slot_grad, own_grad = carry
        query_block = lax.dynamic_index_in_dim(whole_queries, block_index, 0, keepdims=False)
        logits = scores(block_index, query_block)
        row_lse = lax.dynamic_index_in_dim(query_lse, block_index, 0, keepdims=False)
        col_lse = lax.dynamic_index_in_dim(cand_lse, block_index, 0, keepdims=False)
        probs = (
            0.5 * jnp.exp(logits - row_lse[None, :])
            + 0.5 * jnp.exp(logits - col_lse[:, None])
            - target
        )
        rounded = probs.astype(jnp.bfloat16)
        passage_part = jnp.einsum(
            "cr,rd->cd", rounded, query_block, preferred_element_type=jnp.float32
        )
        own_grad = lax.dynamic_update_index_in_dim(
            own_grad, passage_part[:slice_rows], block_index, 0
        )
        slot_targets = lax.dynamic_index_in_dim(slot_of, block_index, 0, keepdims=False)
        slot_grad = slot_grad.at[slot_targets].add(
            passage_part[slice_rows:].reshape(pick_count, slice_rows, embed_width)
        )
        weights = lax.dynamic_update_index_in_dim(weights, rounded, block_index, 0)
        return (weights, slot_grad, own_grad)

    start_carry = (
        jnp.zeros((per_group, cand_rows, full_rows), jnp.bfloat16),
        jnp.zeros((slot_count, slice_rows, embed_width), jnp.float32),
        jnp.zeros((per_group, slice_rows, embed_width), jnp.float32),
    )
    weights, slot_grad, own_grad = lax.fori_loop(0, per_group, backward, start_carry)

    def one_block(inputs):
        block_index, block_weights = inputs
        return jnp.einsum(
            "cr,cd->rd", block_weights, candidates(block_index), preferred_element_type=jnp.float32
        )

    query_sum = lax.psum_scatter(
        jnp.swapaxes(lax.map(one_block, (block_ids, weights)), 0, 1).astype(jnp.bfloat16),
        "inner",
        scatter_dimension=0,
        tiled=True,
    ).astype(jnp.float32)
    query_grad = jnp.swapaxes(query_sum, 0, 1).astype(jnp.bfloat16)
    returned = lax.all_to_all(
        slot_grad.astype(jnp.bfloat16).reshape(groups, CAP, slice_rows, embed_width),
        "dp",
        split_axis=0,
        concat_axis=0,
        tiled=True,
    )
    passage_sum = jnp.einsum(
        "eg,ecd->gcd",
        belongs.astype(jnp.bfloat16),
        returned.reshape(slot_count, slice_rows, embed_width),
        preferred_element_type=jnp.float32,
    )
    passage_grad = (passage_sum + own_grad).astype(jnp.bfloat16)
    return (mean_loss, query_grad, passage_grad)


def solution(mesh):
    in_specs = (P("dp", "inner", None), P("dp", "inner", None), P())
    out_specs = (P(), P("dp", "inner", None), P("dp", "inner", None))
    return jax.shard_map(body, mesh=mesh, in_specs=in_specs, out_specs=out_specs, check_vma=False)
```

profile of v0, /device:TPU:1, one launch (start us, length us, event | category | flops | bytes accessed | tf_op | source)
XLA Modules:
  0.0 454.0 jit_solution(6817125540954745259)
XLA Ops:
  13.2 70.7 %all-gather.3.cloned.1.call-done = bf16[64,64,1024]{2,1,0:T(8,128)(2,1)} async-done(((bf16[4,64,1024]{2,1,0:T(8,128)(2,1)}), bf16[64,64,1024]{2,1,0:T(8,128)(2,1)}) %all-gather.3.cloned.1.call-update) | async-done | bytes 8388624 | tf_op jit(solution)/shard_map/all_gather | solution.py:47
  83.9 6.1 %gather_fusion = bf16[32,64,1024]{2,1,0:T(8,128)(2,1)} fusion(bf16[64,64,1024]{2,1,0:T(8,128)(2,1)} %all-gather.3.cloned.1.call-done, s32[1024]{0:T(1024)S(1)} %pad_clamp_fusion.3), kind=kCustom, calls=%fused_computation | custom fusion | bytes 8388736 | tf_op jit(solution)/shard_map/gather | solution.py:49
  90.0 4.5 broadcast_select_fusion
  94.5 23.6 %all-gather.5.cloned.1.call-done = bf16[4,512,1024]{2,1,0:T(8,128)(2,1)} async-done(((bf16[4,64,1024]{2,1,0:T(8,128)(2,1)}), bf16[4,512,1024]{2,1,0:T(8,128)(2,1)}) %all-gather.5.cloned.1.call-update) | async-done | bytes 4194320 | tf_op jit(solution)/shard_map/all_gather | solution.py:51
  118.2 27.3 %while.44 = (s32[]{:T(128)}, f32[4,512]{1,0:T(4,128)S(1)}, f32[4,512]{1,0:T(4,128)S(1)}, f32[4,576]{1,0:T(4,128)S(1)}, f32[4,576]{1,0:T(4,128)S(1)}, /*index=5*/...) while((s32[]{:T(128)}, f32[4,512]{1,0:T(4,128)S(1)}, ...), condition=%wide.region_5.6_spmd, body=%wide.region_0.5_spmd.sunk | while | flops 606631808 | bytes 9346491 | solution.py:78
  147.6 6.5 %all-to-all-start.1 = ((f32[16,1,128]{2,1,0:T(1,128)}), f32[16,1,128]{2,1,0:T(1,128)S(1)}, u32[]{:S(2)}, u32[]{:S(2)}) async-start(f32[16,1,128]{2,1,0:T(1,128)} %reshape.334), calls=%async_computation.1 | async-start | bytes 16384 | tf_op jit(solution)/shard_map/all_to_all | solution.py:99
  154.8 12.5 %pmax.7 = f32[4,512]{1,0:T(4,128)S(1)} all-reduce(f32[4,512]{1,0:T(4,128)S(1)} %get-tuple-element.271), channel_id=1, replica_groups=mesh['dp'=16,'inner'=8] {'inner'}, use_global_device_ids=true, to_apply=%region_6.7 | all-reduce | flops 2048 | bytes 16384 | tf_op jit(solution)/shard_map/pmax | solution.py:79
  167.3 13.3 %psum.14 = f32[4,512]{1,0:T(4,128)S(1)} all-reduce(f32[4,512]{1,0:T(4,128)S(1)} %exponential_multiply_fusion.1), channel_id=1, replica_groups=mesh['dp'=16,'inner'=8] {'inner'}, use_global_device_ids=true, to_apply=%region_7.8 | all-reduce | flops 2048 | bytes 16384 | tf_op jit(solution)/shard_map/psum | solution.py:80
  180.7 6.4 %all-to-all-start = ((f32[16,1,128]{2,1,0:T(1,128)}), f32[16,1,128]{2,1,0:T(1,128)S(1)}, u32[]{:S(2)}, u32[]{:S(2)}) async-start(f32[16,1,128]{2,1,0:T(1,128)} %reshape.332), calls=%async_computation | async-start | bytes 16384 | tf_op jit(solution)/shard_map/all_to_all | solution.py:92
  188.3 5.1 %all-to-all-done = f32[16,1,128]{2,1,0:T(1,128)S(1)} async-done(((f32[16,1,128]{2,1,0:T(1,128)}), f32[16,1,128]{2,1,0:T(1,128)S(1)}, u32[]{:S(2)}, u32[]{:S(2)}) %all-to-all-start) | async-done | bytes 8224 | tf_op jit(solution)/shard_map/all_to_all | solution.py:92
  196.4 3.5 all-to-all-start.2
  200.1 6.0 %all-to-all-done.2 = f32[16,1,128]{2,1,0:T(1,128)S(1)} async-done(((f32[16,1,128]{2,1,0:T(1,128)}), f32[16,1,128]{2,1,0:T(1,128)S(1)}, u32[]{:S(2)}, u32[]{:S(2)}) %all-to-all-start.2) | async-done | bytes 8224 | tf_op jit(solution)/shard_map/all_to_all | solution.py:128
  207.6 4.3 broadcast_in_dim.183
  211.9 72.2 %while.46 = (s32[]{:T(128)}, bf16[4,576,512]{2,1,0:T(8,128)(2,1)}, f32[32,64,1024]{2,1,0:T(8,128)}, f32[4,64,1024]{2,0,1:T(4,128)}, bf16[4,64,1024]{2,1,0:T(8,12...) while((s32[]{:T(128)}, bf16[4,576,512]{2,1,0:T(8,128)(2,1)}, ...), condition=%wide.region_21.22_spmd.clone, body=%wide.region_19.21_spmd.clone.sunk | while | flops 1212022784 | bytes 40981276 | solution.py:171
  218.6 5.1 %scatter_fusion = f32[32,64,1024]{2,1,0:T(8,128)} fusion(f32[32,64,1024]{2,1,0:T(8,128)} %get-tuple-element.624, s32[8]{0:T(128)S(1)} %fusion.79, f32[8,64,1024]{2,1,0:T(8,128)} %bitcast.138), kind=kCustom, calls=%fused_computation.5.clone.clone.1 | custom fusion | flops 524288 | bytes 6291488 | tf_op jit(solution)/shard_map/while/body/eval_jaxpr/scatter-add | solution.py:160
  224.0 5.8 %dynamic_update_slice.51 = f32[4,64,1024]{2,0,1:T(4,128)} dynamic-update-slice(f32[4,64,1024]{2,0,1:T(4,128)} %get-tuple-element.625, f32[1,64,1024]{2,0,1:T(1,128)S(1)} %copy.96, s32[]{:T(128)} %get-tuple-element.622, s32[]{:T(128)} %constant.189.clone.1..sunk.2, s32[]{:T(128)} %constant.189.clone.1..sunk.2) | dynamic-update-slice | bytes 524292 | tf_op jit(solution)/shard_map/while/body/eval_jaxpr/jit(dynamic_update_index_in_dim)/dynamic_update_slice | solution.py:156
  236.6 5.2 %scatter_fusion = f32[32,64,1024]{2,1,0:T(8,128)} fusion(f32[32,64,1024]{2,1,0:T(8,128)} %get-tuple-element.624, s32[8]{0:T(128)S(1)} %fusion.79, f32[8,64,1024]{2,1,0:T(8,128)} %bitcast.138), kind=kCustom, calls=%fused_computation.5.clone.clone.1 | custom fusion | flops 524288 | bytes 6291488 | tf_op jit(solution)/shard_map/while/body/eval_jaxpr/scatter-add | solution.py:160
  242.1 5.8 %dynamic_update_slice.51 = f32[4,64,1024]{2,0,1:T(4,128)} dynamic-update-slice(f32[4,64,1024]{2,0,1:T(4,128)} %get-tuple-element.625, f32[1,64,1024]{2,0,1:T(1,128)S(1)} %copy.96, s32[]{:T(128)} %get-tuple-element.622, s32[]{:T(128)} %constant.189.clone.1..sunk.2, s32[]{:T(128)} %constant.189.clone.1..sunk.2) | dynamic-update-slice | bytes 524292 | tf_op jit(solution)/shard_map/while/body/eval_jaxpr/jit(dynamic_update_index_in_dim)/dynamic_update_slice | solution.py:156
  254.7 5.1 %scatter_fusion = f32[32,64,1024]{2,1,0:T(8,128)} fusion(f32[32,64,1024]{2,1,0:T(8,128)} %get-tuple-element.624, s32[8]{0:T(128)S(1)} %fusion.79, f32[8,64,1024]{2,1,0:T(8,128)} %bitcast.138), kind=kCustom, calls=%fused_computation.5.clone.clone.1 | custom fusion | flops 524288 | bytes 6291488 | tf_op jit(solution)/shard_map/while/body/eval_jaxpr/scatter-add | solution.py:160
  260.2 5.8 %dynamic_update_slice.51 = f32[4,64,1024]{2,0,1:T(4,128)} dynamic-update-slice(f32[4,64,1024]{2,0,1:T(4,128)} %get-tuple-element.625, f32[1,64,1024]{2,0,1:T(1,128)S(1)} %copy.96, s32[]{:T(128)} %get-tuple-element.622, s32[]{:T(128)} %constant.189.clone.1..sunk.2, s32[]{:T(128)} %constant.189.clone.1..sunk.2) | dynamic-update-slice | bytes 524292 | tf_op jit(solution)/shard_map/while/body/eval_jaxpr/jit(dynamic_update_index_in_dim)/dynamic_update_slice | solution.py:156
  272.8 5.1 %scatter_fusion = f32[32,64,1024]{2,1,0:T(8,128)} fusion(f32[32,64,1024]{2,1,0:T(8,128)} %get-tuple-element.624, s32[8]{0:T(128)S(1)} %fusion.79, f32[8,64,1024]{2,1,0:T(8,128)} %bitcast.138), kind=kCustom, calls=%fused_computation.5.clone.clone.1 | custom fusion | flops 524288 | bytes 6291488 | tf_op jit(solution)/shard_map/while/body/eval_jaxpr/scatter-add | solution.py:160
  278.2 5.8 %dynamic_update_slice.51 = f32[4,64,1024]{2,0,1:T(4,128)} dynamic-update-slice(f32[4,64,1024]{2,0,1:T(4,128)} %get-tuple-element.625, f32[1,64,1024]{2,0,1:T(1,128)S(1)} %copy.96, s32[]{:T(128)} %get-tuple-element.622, s32[]{:T(128)} %constant.189.clone.1..sunk.2, s32[]{:T(128)} %constant.189.clone.1..sunk.2) | dynamic-update-slice | bytes 524292 | tf_op jit(solution)/shard_map/while/body/eval_jaxpr/jit(dynamic_update_index_in_dim)/dynamic_update_slice | solution.py:156
  284.1 28.3 %while.45 = (s32[]{:T(128)}, bf16[4,512,1024]{2,1,0:T(8,128)(2,1)}, bf16[4,576,512]{2,1,0:T(8,128)(2,1)}, s32[4]{0:T(128)S(1)}, bf16[4,64,1024]{2,1,0:T(8,128)(2...) while((s32[]{:T(128)}, bf16[4,512,1024]{2,1,0:T(8,128)(2,1)}, ...), condition=%wide.region_23.24_spmd, body=%wide.region_22.23_spmd.sunk | while | flops 604569600 | bytes 8586387 | solution.py:180
  288.0 3.1 bitcast_dynamic-update-slice_fusion.4
  295.1 3.1 bitcast_dynamic-update-slice_fusion.4
  302.2 3.1 bitcast_dynamic-update-slice_fusion.4
  309.3 3.1 bitcast_dynamic-update-slice_fusion.4
  312.4 4.0 convert_element_type.45
  316.4 6.3 %copy.71 = bf16[16,2,64,1024]{3,1,2,0:T(2,128)(2,1)} copy(bf16[16,2,64,1024]{3,2,1,0:T(8,128)(2,1)S(1)} %bitcast.142) | data formatting | bytes 8388608 | tf_op jit(solution)/shard_map/reshape | solution.py:187
  322.7 4.7 %all-to-all-start.3 = ((bf16[16,2,64,1024]{3,1,2,0:T(2,128)(2,1)}), bf16[16,2,64,1024]{3,1,2,0:T(2,128)(2,1)}, u32[]{:S(2)}, u32[]{:S(2)}) async-start(bf16[16,2,64,1024]{3,1,2,0:T(2,128)(2,1)} %copy.71), calls=%async_computation.4 | async-start | bytes 8388608 | tf_op jit(solution)/shard_map/all_to_all | solution.py:186
  328.7 111.3 %psum.15 = f32[]{:T(128)} all-reduce(f32[]{:T(128)S(6)} %add.200), channel_id=1, replica_groups=mesh['dp'=16,'inner'=8] {'dp','inner'}, use_global_device_ids=true, to_apply=%region_18.19 | all-reduce | flops 1 | bytes 8 | tf_op jit(solution)/shard_map/psum | solution.py:126
  440.6 4.8 %fusion.27 = bf16[4,64,1024]{2,0,1:T(4,128)(2,1)S(1)} fusion(f32[4,64,1024]{2,0,1:T(4,128)S(1)} %copy-done.3, bf16[16,2,64,1024]{3,1,2,0:T(2,128)(2,1)} %all-to-all-done.3, s32[16,2]{0,1:T(2,128)S(1)} %get-tuple-element.386, pred[16,2]{0,1:T(4,128)(4,1)S(1)} %get-tuple-element.382), kind=kOutput, calls=%fused_computation.52 | convolution fusion | flops 17301760 | bytes 5767328 | tf_op jit(solution)/shard_map/eg,ecd->gcd/dot_general | solution.py:193
  (214 shorter events, 70.9 us)
Async XLA Ops:
  7.2 5.7 %copy-start = (bf16[4,64,1024]{2,1,0:T(8,128)(2,1)S(1)}, bf16[4,64,1024]{2,1,0:T(8,128)(2,1)}, u32[]{:S(2)}) copy-start(bf16[4,64,1024]{2,1,0:T(8,128)(2,1)} %param.10) | copy-start | bytes 1572868
  7.2 5.7 %copy-start.2 = (bf16[4,64,1024]{2,1,0:T(8,128)(2,1)S(1)}, bf16[4,64,1024]{2,1,0:T(8,128)(2,1)}, u32[]{:S(2)}) copy-start(bf16[4,64,1024]{2,1,0:T(8,128)(2,1)} %param.9) | copy-start | bytes 1572868
  7.2 76.7 %all-gather.3.cloned.1.call-start = ((), (), s32[]{:S(2)}) async-start(), calls=%async_computation.5 | async-start | bytes 8912896 | tf_op jit(solution)/shard_map/all_gather | solution.py:47
  7.9 110.3 %all-gather.5.cloned.1.call-start = ((), (), s32[]{:S(2)}) async-start(), calls=%async_computation.6 | async-start | bytes 4718592 | tf_op jit(solution)/shard_map/all_gather | solution.py:51
  147.6 33.0 %all-to-all-start.1 = ((f32[16,1,128]{2,1,0:T(1,128)}), f32[16,1,128]{2,1,0:T(1,128)S(1)}, u32[]{:S(2)}, u32[]{:S(2)}) async-start(f32[16,1,128]{2,1,0:T(1,128)} %reshape.334), calls=%async_computation.1 | async-start | bytes 16384 | tf_op jit(solution)/shard_map/all_to_all | solution.py:99
  180.7 12.7 %all-to-all-start = ((f32[16,1,128]{2,1,0:T(1,128)}), f32[16,1,128]{2,1,0:T(1,128)S(1)}, u32[]{:S(2)}, u32[]{:S(2)}) async-start(f32[16,1,128]{2,1,0:T(1,128)} %reshape.332), calls=%async_computation | async-start | bytes 16384 | tf_op jit(solution)/shard_map/all_to_all | solution.py:92
  196.4 9.8 %all-to-all-start.2 = ((f32[16,1,128]{2,1,0:T(1,128)}), f32[16,1,128]{2,1,0:T(1,128)S(1)}, u32[]{:S(2)}, u32[]{:S(2)}) async-start(f32[16,1,128]{2,1,0:T(1,128)} %reshape.336), calls=%async_computation.2 | async-start | bytes 16384 | tf_op jit(solution)/shard_map/all_to_all | solution.py:128
  199.8 246.5 %reduce-scatter.2.cloned.1.call-start = ((), (), s32[]{:S(2)}) async-start(), calls=%async_computation.7 | async-start | bytes 4718592 | tf_op jit(solution)/shard_map/reduce_scatter | solution.py:179
  211.9 2.5 copy-start.1
  229.9 2.5 copy-start.1
  247.9 2.5 copy-start.1
  266.0 2.5 copy-start.1
  322.7 117.9 %copy-start.3 = (f32[4,64,1024]{2,0,1:T(4,128)S(1)}, f32[4,64,1024]{2,0,1:T(4,128)}, u32[]{:S(2)}) copy-start(f32[4,64,1024]{2,0,1:T(4,128)} %get-tuple-element.278) | copy-start | bytes 3145732
  322.7 117.9 %all-to-all-start.3 = ((bf16[16,2,64,1024]{3,1,2,0:T(2,128)(2,1)}), bf16[16,2,64,1024]{3,1,2,0:T(2,128)(2,1)}, u32[]{:S(2)}, u32[]{:S(2)}) async-start(bf16[16,2,64,1024]{3,1,2,0:T(2,128)(2,1)} %copy.71), calls=%async_computation.4 | async-start | bytes 8388608 | tf_op jit(solution)/shard_map/all_to_all | solution.py:186
Sparse Core Ops, SparseCore 0:
  10.1 73.7 all-gather.2
  85.6 32.5 all-gather.4
  312.5 33.4 reduce-scatter.1
where the time goes:
time: 456 us; the launch traced here: 454 us
  blocking collectives  137 us (30%)
  waiting for transfers between devices  107 us (23%)
  local copies, waits for them, and re-layouts  82.3 us (18%)
  matrix products  37 us (8%)
  other arithmetic  36.1 us (8%)
  starting transfers between devices  21.3 us (5%)
  between operations  17.2 us (4%)
  loops' own time  16.1 us (4%)
    psum x1, blocking collectives, body(): lax.psum(local_loss, ('dp', 'inner'))  111 us
    all_gather x1, waiting for transfers between devices, body(): shard_rows = lax.all_gather(passages, 'dp', axis=0, tiled=True)  70.7 us
    dynamic_update_slice x8, local copies, waits for them, and re-layouts, backward(): lax.dynamic_update_index_in_dim(own_grad, passage_part[:slice_rows], bloc...  24.4 us
    all_gather x1, waiting for transfers between devices, body(): whole_queries = lax.all_gather(queries, 'inner', axis=1, tiled=True)  23.6 us
    scatter-add x4, other arithmetic, backward(): slot_grad.at[slot_targets]  20.5 us
    dot_general x8, matrix products, scores(): jnp.einsum('cd,rd->cr', candidates(block_index), query_block, preferred_e...  16.6 us
    squeeze x12, local copies, waits for them, and re-layouts, candidates(): lax.dynamic_index_in_dim(negatives, block_index, 0, keepdims=False)  16.3 us
    psum x1, blocking collectives, body(): mass_all = lax.psum(row_mass * jnp.exp(row_peak - peak_all), 'inner')  13.3 us
  transfers between devices with their start and end apart: 7, of which 4 were waited for; matrix products, arithmetic and copies ran while one was open for 7% of the time, Pallas kernels for 0%

commit v1 on v0

--- a/solution.py
+++ b/solution.py
@@ -48,7 +48,9 @@
     inside = (listed >= 0) & (listed < shard_rows.shape[0])
     picked = shard_rows[jnp.clip(listed, 0, shard_rows.shape[0] - 1)]
     negatives = jnp.where(inside[:, :, None, None], picked, held_start)
-    whole_queries = lax.all_gather(queries, "inner", axis=1, tiled=True)
+    whole_queries = jnp.concatenate(
+        lax.all_to_all(jnp.stack([queries] * lax.axis_size("inner")), "inner", 0, 0), axis=1
+    )
 
     def candidates(block_index):
         own_rows = lax.dynamic_index_in_dim(passages, block_index, 0, keepdims=True)

time: 456 us -> 433 us (0.950)
  waiting for transfers between devices: 107 us -> 68.4 us
  local copies, waits for them, and re-layouts: 82.3 us -> 90.1 us
  starting transfers between devices: 21.3 us -> 26.7 us
    all_gather x1, waiting for transfers between devices: 70.7 us -> 11.7 us  [body(): shard_rows = lax.all_gather(passages, 'dp', axis=0, tiled=True)]
    all_to_all x0 -> x1, waiting for transfers between devices: none -> 44.9 us  [body(): lax.all_to_all(jnp.stack([queries] * lax.axis_size('inner')), 'inner', 0, 0)]
    all_gather x1 -> x0, waiting for transfers between devices: 23.6 us -> none  [body(): whole_queries = lax.all_gather(queries, 'inner', axis=1, tiled=True)]
    all_to_all x0 -> x1, starting transfers between devices: none -> 6.93 us  [body(): lax.all_to_all(jnp.stack([queries] * lax.axis_size('inner')), 'inner', 0, 0)]
    all_to_all x0 -> x1, local copies, waits for them, and re-layouts: none -> 5.01 us  [body(): lax.all_to_all(jnp.stack([queries] * lax.axis_size('inner')), 'inner', 0, 0)]
where the time goes in v1:
time: 433 us; the launch traced here: 431 us
  blocking collectives  139 us (32%)
  local copies, waits for them, and re-layouts  90.1 us (21%)
  waiting for transfers between devices  68.4 us (16%)
  matrix products  37 us (9%)
  other arithmetic  36.1 us (8%)
  starting transfers between devices  26.7 us (6%)
  between operations  17.5 us (4%)
  loops' own time  16.1 us (4%)
    psum x1, blocking collectives, body(): lax.psum(local_loss, ('dp', 'inner'))  111 us
    all_to_all x1, waiting for transfers between devices, body(): lax.all_to_all(jnp.stack([queries] * lax.axis_size('inner')), 'inner', 0, 0)  44.9 us
    dynamic_update_slice x8, local copies, waits for them, and re-layouts, backward(): lax.dynamic_update_index_in_dim(own_grad, passage_part[:slice_rows], bloc...  24.4 us
    scatter-add x4, other arithmetic, backward(): slot_grad.at[slot_targets]  20.5 us
    dot_general x8, matrix products, scores(): jnp.einsum('cd,rd->cr', candidates(block_index), query_block, preferred_e...  16.6 us
    squeeze x12, local copies, waits for them, and re-layouts, candidates(): lax.dynamic_index_in_dim(negatives, block_index, 0, keepdims=False)  16.3 us
    psum x1, blocking collectives, body(): mass_all = lax.psum(row_mass * jnp.exp(row_peak - peak_all), 'inner')  14.8 us
    pmax x1, blocking collectives, body(): peak_all = lax.pmax(row_peak, 'inner')  13.2 us
  transfers between devices with their start and end apart: 7, of which 4 were waited for; matrix products, arithmetic and copies ran while one was open for 7% of the time, Pallas kernels for 0%

profile of v1, /device:TPU:1, one launch (start us, length us, event | category | flops | bytes accessed | tf_op | source)
XLA Modules:
  0.0 431.2 jit_solution(17603329458877102932)
XLA Ops:
  7.9 3.5 stack.2
  11.4 6.9 %all-to-all-start = ((bf16[8,4,64,1024]{3,2,1,0:T(8,128)(2,1)}), bf16[8,4,64,1024]{3,2,1,0:T(8,128)(2,1)}, u32[]{:S(2)}, u32[]{:S(2)}) async-start(bf16[8,4,64,1024]{3,2,1,0:T(8,128)(2,1)} %stack.2), calls=%async_computation | async-start | bytes 8388608 | tf_op jit(solution)/shard_map/all_to_all | solution.py:52
  22.3 44.9 %all-to-all-done = bf16[8,4,64,1024]{3,2,1,0:T(8,128)(2,1)} async-done(((bf16[8,4,64,1024]{3,2,1,0:T(8,128)(2,1)}), bf16[8,4,64,1024]{3,2,1,0:T(8,128)(2,1)}, u32[]{:S(2)}, u32[]{:S(2)}) %all-to-all-start) | async-done | bytes 4194336 | tf_op jit(solution)/shard_map/all_to_all | solution.py:52
  67.2 5.0 %copy.76 = bf16[8,4,64,1024]{3,2,0,1:T(8,128)(2,1)} copy(bf16[8,4,64,1024]{3,2,1,0:T(8,128)(2,1)} %all-to-all-done) | data formatting | bytes 8388608 | tf_op jit(solution)/shard_map/all_to_all | solution.py:52
  72.2 11.7 %all-gather.2.cloned.1.call-done = bf16[64,64,1024]{2,1,0:T(8,128)(2,1)} async-done(((bf16[4,64,1024]{2,1,0:T(8,128)(2,1)}), bf16[64,64,1024]{2,1,0:T(8,128)(2,1)}) %all-gather.2.cloned.1.call-update) | async-done | bytes 8388624 | tf_op jit(solution)/shard_map/all_gather | solution.py:47
  83.8 6.1 %gather_fusion = bf16[32,64,1024]{2,1,0:T(8,128)(2,1)} fusion(bf16[64,64,1024]{2,1,0:T(8,128)(2,1)} %all-gather.2.cloned.1.call-done, s32[1024]{0:T(1024)S(1)} %pad_clamp_fusion.3), kind=kCustom, calls=%fused_computation | custom fusion | bytes 8388736 | tf_op jit(solution)/shard_map/gather | solution.py:49
  90.0 4.5 %broadcast_select_fusion = bf16[4,8,64,1024]{3,2,1,0:T(8,128)(2,1)} fusion(bf16[4,8,64,1024]{3,2,1,0:T(8,128)(2,1)} %bitcast.147, pred[4,8]{1,0:T(4,128)(4,1)S(1)} %compare_and_fusion), kind=kLoop, calls=%fused_computation.49 | loop fusion | flops 2097152 | bytes 8388640 | tf_op jit(solution)/shard_map/jit(_where)/select_n | solution.py:50
  94.5 27.3 %while.44 = (s32[]{:T(128)}, f32[4,512]{1,0:T(4,128)S(1)}, f32[4,512]{1,0:T(4,128)S(1)}, f32[4,576]{1,0:T(4,128)S(1)}, f32[4,576]{1,0:T(4,128)S(1)}, /*index=5*/...) while((s32[]{:T(128)}, f32[4,512]{1,0:T(4,128)S(1)}, ...), condition=%wide.region_5.6_spmd, body=%wide.region_0.5_spmd.sunk | while | flops 606631808 | bytes 9346491 | solution.py:80
  123.9 5.0 %all-to-all-start.2 = ((f32[16,1,128]{2,1,0:T(1,128)}), f32[16,1,128]{2,1,0:T(1,128)S(1)}, u32[]{:S(2)}, u32[]{:S(2)}) async-start(f32[16,1,128]{2,1,0:T(1,128)} %reshape.344), calls=%async_computation.2 | async-start | bytes 16384 | tf_op jit(solution)/shard_map/all_to_all | solution.py:101
  129.5 13.2 %pmax.7 = f32[4,512]{1,0:T(4,128)S(1)} all-reduce(f32[4,512]{1,0:T(4,128)S(1)} %get-tuple-element.271), channel_id=1, replica_groups=mesh['dp'=16,'inner'=8] {'inner'}, use_global_device_ids=true, to_apply=%region_6.7 | all-reduce | flops 2048 | bytes 16384 | tf_op jit(solution)/shard_map/pmax | solution.py:81
  142.7 14.8 %psum.14 = f32[4,512]{1,0:T(4,128)S(1)} all-reduce(f32[4,512]{1,0:T(4,128)S(1)} %exponential_multiply_fusion.1), channel_id=1, replica_groups=mesh['dp'=16,'inner'=8] {'inner'}, use_global_device_ids=true, to_apply=%region_7.8 | all-reduce | flops 2048 | bytes 16384 | tf_op jit(solution)/shard_map/psum | solution.py:82
  157.6 6.4 %all-to-all-start.1 = ((f32[16,1,128]{2,1,0:T(1,128)}), f32[16,1,128]{2,1,0:T(1,128)S(1)}, u32[]{:S(2)}, u32[]{:S(2)}) async-start(f32[16,1,128]{2,1,0:T(1,128)} %reshape.342), calls=%async_computation.1 | async-start | bytes 16384 | tf_op jit(solution)/shard_map/all_to_all | solution.py:94
  165.2 5.1 %all-to-all-done.1 = f32[16,1,128]{2,1,0:T(1,128)S(1)} async-done(((f32[16,1,128]{2,1,0:T(1,128)}), f32[16,1,128]{2,1,0:T(1,128)S(1)}, u32[]{:S(2)}, u32[]{:S(2)}) %all-to-all-start.1) | async-done | bytes 8224 | tf_op jit(solution)/shard_map/all_to_all | solution.py:94
  173.3 3.5 all-to-all-start.3
  177.0 6.0 %all-to-all-done.3 = f32[16,1,128]{2,1,0:T(1,128)S(1)} async-done(((f32[16,1,128]{2,1,0:T(1,128)}), f32[16,1,128]{2,1,0:T(1,128)S(1)}, u32[]{:S(2)}, u32[]{:S(2)}) %all-to-all-start.3) | async-done | bytes 8224 | tf_op jit(solution)/shard_map/all_to_all | solution.py:130
  184.5 4.3 broadcast_in_dim.183
  188.8 72.2 %while.46 = (s32[]{:T(128)}, bf16[4,576,512]{2,1,0:T(8,128)(2,1)}, f32[32,64,1024]{2,1,0:T(8,128)}, f32[4,64,1024]{2,0,1:T(4,128)}, bf16[4,64,1024]{2,1,0:T(8,12...) while((s32[]{:T(128)}, bf16[4,576,512]{2,1,0:T(8,128)(2,1)}, ...), condition=%wide.region_21.22_spmd.clone, body=%wide.region_19.21_spmd.clone.sunk | while | flops 1212022784 | bytes 40981276 | solution.py:173
  195.5 5.1 %scatter_fusion = f32[32,64,1024]{2,1,0:T(8,128)} fusion(f32[32,64,1024]{2,1,0:T(8,128)} %get-tuple-element.627, s32[8]{0:T(128)S(1)} %fusion.79, f32[8,64,1024]{2,1,0:T(8,128)} %bitcast.141), kind=kCustom, calls=%fused_computation.5.clone.clone.1 | custom fusion | flops 524288 | bytes 6291488 | tf_op jit(solution)/shard_map/while/body/eval_jaxpr/scatter-add | solution.py:162
  200.9 5.8 %dynamic_update_slice.51 = f32[4,64,1024]{2,0,1:T(4,128)} dynamic-update-slice(f32[4,64,1024]{2,0,1:T(4,128)} %get-tuple-element.628, f32[1,64,1024]{2,0,1:T(1,128)S(1)} %copy.113, s32[]{:T(128)} %get-tuple-element.625, s32[]{:T(128)} %constant.189.clone.1..sunk.2, s32[]{:T(128)} %constant.189.clone.1..sunk.2) | dynamic-update-slice | bytes 524292 | tf_op jit(solution)/shard_map/while/body/eval_jaxpr/jit(dynamic_update_index_in_dim)/dynamic_update_slice | solution.py:158
  213.5 5.2 %scatter_fusion = f32[32,64,1024]{2,1,0:T(8,128)} fusion(f32[32,64,1024]{2,1,0:T(8,128)} %get-tuple-element.627, s32[8]{0:T(128)S(1)} %fusion.79, f32[8,64,1024]{2,1,0:T(8,128)} %bitcast.141), kind=kCustom, calls=%fused_computation.5.clone.clone.1 | custom fusion | flops 524288 | bytes 6291488 | tf_op jit(solution)/shard_map/while/body/eval_jaxpr/scatter-add | solution.py:162
  219.0 5.8 %dynamic_update_slice.51 = f32[4,64,1024]{2,0,1:T(4,128)} dynamic-update-slice(f32[4,64,1024]{2,0,1:T(4,128)} %get-tuple-element.628, f32[1,64,1024]{2,0,1:T(1,128)S(1)} %copy.113, s32[]{:T(128)} %get-tuple-element.625, s32[]{:T(128)} %constant.189.clone.1..sunk.2, s32[]{:T(128)} %constant.189.clone.1..sunk.2) | dynamic-update-slice | bytes 524292 | tf_op jit(solution)/shard_map/while/body/eval_jaxpr/jit(dynamic_update_index_in_dim)/dynamic_update_slice | solution.py:158
  231.6 5.1 %scatter_fusion = f32[32,64,1024]{2,1,0:T(8,128)} fusion(f32[32,64,1024]{2,1,0:T(8,128)} %get-tuple-element.627, s32[8]{0:T(128)S(1)} %fusion.79, f32[8,64,1024]{2,1,0:T(8,128)} %bitcast.141), kind=kCustom, calls=%fused_computation.5.clone.clone.1 | custom fusion | flops 524288 | bytes 6291488 | tf_op jit(solution)/shard_map/while/body/eval_jaxpr/scatter-add | solution.py:162
  237.1 5.8 %dynamic_update_slice.51 = f32[4,64,1024]{2,0,1:T(4,128)} dynamic-update-slice(f32[4,64,1024]{2,0,1:T(4,128)} %get-tuple-element.628, f32[1,64,1024]{2,0,1:T(1,128)S(1)} %copy.113, s32[]{:T(128)} %get-tuple-element.625, s32[]{:T(128)} %constant.189.clone.1..sunk.2, s32[]{:T(128)} %constant.189.clone.1..sunk.2) | dynamic-update-slice | bytes 524292 | tf_op jit(solution)/shard_map/while/body/eval_jaxpr/jit(dynamic_update_index_in_dim)/dynamic_update_slice | solution.py:158
  249.7 5.1 %scatter_fusion = f32[32,64,1024]{2,1,0:T(8,128)} fusion(f32[32,64,1024]{2,1,0:T(8,128)} %get-tuple-element.627, s32[8]{0:T(128)S(1)} %fusion.79, f32[8,64,1024]{2,1,0:T(8,128)} %bitcast.141), kind=kCustom, calls=%fused_computation.5.clone.clone.1 | custom fusion | flops 524288 | bytes 6291488 | tf_op jit(solution)/shard_map/while/body/eval_jaxpr/scatter-add | solution.py:162
  255.1 5.8 %dynamic_update_slice.51 = f32[4,64,1024]{2,0,1:T(4,128)} dynamic-update-slice(f32[4,64,1024]{2,0,1:T(4,128)} %get-tuple-element.628, f32[1,64,1024]{2,0,1:T(1,128)S(1)} %copy.113, s32[]{:T(128)} %get-tuple-element.625, s32[]{:T(128)} %constant.189.clone.1..sunk.2, s32[]{:T(128)} %constant.189.clone.1..sunk.2) | dynamic-update-slice | bytes 524292 | tf_op jit(solution)/shard_map/while/body/eval_jaxpr/jit(dynamic_update_index_in_dim)/dynamic_update_slice | solution.py:158
  261.0 28.3 %while.45 = (s32[]{:T(128)}, bf16[4,512,1024]{2,1,0:T(8,128)(2,1)}, bf16[4,576,512]{2,1,0:T(8,128)(2,1)}, s32[4]{0:T(128)S(1)}, bf16[4,64,1024]{2,1,0:T(8,128)(2...) while((s32[]{:T(128)}, bf16[4,512,1024]{2,1,0:T(8,128)(2,1)}, ...), condition=%wide.region_23.24_spmd, body=%wide.region_22.23_spmd.sunk | while | flops 604569600 | bytes 8586387 | solution.py:182
  272.0 3.1 bitcast_dynamic-update-slice_fusion.4
  289.3 4.0 convert_element_type.45
  293.3 6.3 %copy.88 = bf16[16,2,64,1024]{3,1,2,0:T(2,128)(2,1)} copy(bf16[16,2,64,1024]{3,2,1,0:T(8,128)(2,1)S(1)} %bitcast.146) | data formatting | bytes 8388608 | tf_op jit(solution)/shard_map/reshape | solution.py:189
  299.6 4.7 %all-to-all-start.4 = ((bf16[16,2,64,1024]{3,1,2,0:T(2,128)(2,1)}), bf16[16,2,64,1024]{3,1,2,0:T(2,128)(2,1)}, u32[]{:S(2)}, u32[]{:S(2)}) async-start(bf16[16,2,64,1024]{3,1,2,0:T(2,128)(2,1)} %copy.88), calls=%async_computation.5 | async-start | bytes 8388608 | tf_op jit(solution)/shard_map/all_to_all | solution.py:188
  305.6 111.3 %psum.15 = f32[]{:T(128)} all-reduce(f32[]{:T(128)S(6)} %add.200), channel_id=1, replica_groups=mesh['dp'=16,'inner'=8] {'dp','inner'}, use_global_device_ids=true, to_apply=%region_18.19 | all-reduce | flops 1 | bytes 8 | tf_op jit(solution)/shard_map/psum | solution.py:128
  417.5 4.8 %fusion.27 = bf16[4,64,1024]{2,0,1:T(4,128)(2,1)S(1)} fusion(f32[4,64,1024]{2,0,1:T(4,128)S(1)} %copy-done.3, bf16[16,2,64,1024]{3,1,2,0:T(2,128)(2,1)} %all-to-all-done.4, s32[16,2]{0,1:T(2,128)S(1)} %get-tuple-element.389, pred[16,2]{0,1:T(4,128)(4,1)S(1)} %get-tuple-element.385), kind=kOutput, calls=%fused_computation.52 | convolution fusion | flops 17301760 | bytes 5767328 | tf_op jit(solution)/shard_map/eg,ecd->gcd/dot_general | solution.py:195
  (217 shorter events, 78.7 us)
Async XLA Ops:
  7.2 76.7 %all-gather.2.cloned.1.call-start = ((), (), s32[]{:S(2)}) async-start(), calls=%async_computation.6 | async-start | bytes 8912896 | tf_op jit(solution)/shard_map/all_gather | solution.py:47
  11.4 7.0 %copy-start.4 = (s32[64,8]{0,1:T(8,128)S(1)}, s32[64,8]{0,1:T(8,128)}, u32[]{:S(2)}) copy-start(s32[64,8]{0,1:T(8,128)} %param.11) | copy-start | bytes 6148
  11.4 55.7 %all-to-all-start = ((bf16[8,4,64,1024]{3,2,1,0:T(8,128)(2,1)}), bf16[8,4,64,1024]{3,2,1,0:T(8,128)(2,1)}, u32[]{:S(2)}, u32[]{:S(2)}) async-start(bf16[8,4,64,1024]{3,2,1,0:T(8,128)(2,1)} %stack.2), calls=%async_computation | async-start | bytes 8388608 | tf_op jit(solution)/shard_map/all_to_all | solution.py:52
  18.4 3.6 copy-start.1
  18.4 3.6 copy-start.2
  123.9 33.7 %all-to-all-start.2 = ((f32[16,1,128]{2,1,0:T(1,128)}), f32[16,1,128]{2,1,0:T(1,128)S(1)}, u32[]{:S(2)}, u32[]{:S(2)}) async-start(f32[16,1,128]{2,1,0:T(1,128)} %reshape.344), calls=%async_computation.2 | async-start | bytes 16384 | tf_op jit(solution)/shard_map/all_to_all | solution.py:101
  157.6 12.7 %all-to-all-start.1 = ((f32[16,1,128]{2,1,0:T(1,128)}), f32[16,1,128]{2,1,0:T(1,128)S(1)}, u32[]{:S(2)}, u32[]{:S(2)}) async-start(f32[16,1,128]{2,1,0:T(1,128)} %reshape.342), calls=%async_computation.1 | async-start | bytes 16384 | tf_op jit(solution)/shard_map/all_to_all | solution.py:94
  173.3 9.8 %all-to-all-start.3 = ((f32[16,1,128]{2,1,0:T(1,128)}), f32[16,1,128]{2,1,0:T(1,128)S(1)}, u32[]{:S(2)}, u32[]{:S(2)}) async-start(f32[16,1,128]{2,1,0:T(1,128)} %reshape.346), calls=%async_computation.3 | async-start | bytes 16384 | tf_op jit(solution)/shard_map/all_to_all | solution.py:130
  176.7 246.5 %reduce-scatter.2.cloned.1.call-start = ((), (), s32[]{:S(2)}) async-start(), calls=%async_computation.7 | async-start | bytes 4718592 | tf_op jit(solution)/shard_map/reduce_scatter | solution.py:181
  188.8 2.5 copy-start
  206.8 2.5 copy-start
  224.8 2.5 copy-start
  242.9 2.5 copy-start
  299.6 117.9 %copy-start.3 = (f32[4,64,1024]{2,0,1:T(4,128)S(1)}, f32[4,64,1024]{2,0,1:T(4,128)}, u32[]{:S(2)}) copy-start(f32[4,64,1024]{2,0,1:T(4,128)} %get-tuple-element.278) | copy-start | bytes 3145732
  299.6 117.9 %all-to-all-start.4 = ((bf16[16,2,64,1024]{3,1,2,0:T(2,128)(2,1)}), bf16[16,2,64,1024]{3,1,2,0:T(2,128)(2,1)}, u32[]{:S(2)}, u32[]{:S(2)}) async-start(bf16[16,2,64,1024]{3,1,2,0:T(2,128)(2,1)} %copy.88), calls=%async_computation.5 | async-start | bytes 8388608 | tf_op jit(solution)/shard_map/all_to_all | solution.py:188
Sparse Core Ops, SparseCore 0:
  10.1 73.6 all-gather.1
  289.4 33.4 reduce-scatter.1
